TPU v7x, 256 devices: a whole 4x4x8 slice. The times are simulated.
256 devices in a mesh: pool: 8 (over z), tp: 32 (over x, y, core).
Axes of the slice: x: 4, y: 4, z: 8, core: 2. Of those that a mesh axis runs over, the one named last changes fastest.
Arguments:
- tokens: bfloat16 [4096, 8192], P(('pool', 'tp')), may hold values from -4 to 4
- lengths: int32 [8, 4], P('pool'), may hold values from 1 to 256, 512 in all within a row
- hit_pages: int32 [8, 4, 4], P('pool'), may hold values from 0 to 4095, as said below
- new_owner: int32 [8, 16], P('pool'), may hold values from 0 to 7, as said below
- w_query: bfloat16 [8192, 8192], P('pool', 'tp'), may hold values from -0.125 to 0.125
- w_keyval: bfloat16 [4096, 4096], P('pool', 'tp'), may hold values from -0.0625 to 0.0625
- w_out: bfloat16 [8192, 8192], P('tp', 'pool'), may hold values from -0.0625 to 0.0625
- pool_pages: bfloat16 [4096, 32, 2048], P('pool', 'tp'), may hold values from -65 to 65
Outputs:
- mixed: float32 [4096, 8192], P(('pool', 'tp'))
- new_store: bfloat16 [128, 32, 2048], P('pool', 'tp')
Inputs may be any that keep to these rules, and one draw needn't show every extreme that they name: Page p of the pool lies on pool index p // 512. In every group g at most 6 of the 16 entries of hit_pages[g] lie on one pool index, and some pool index holds exactly 6 of them in every group. A page may appear more than once. `new_owner`: in every group at most 2 of its 16 pages go to one pool index, and some pool index receives exactly 2 from every group. Row g holds the lengths of the 4 requests packed in group g, in order, and sums to 512.
All inputs are finite; a program needn't handle non-finite values.
Results may differ from a plain program's by a relative error of at most 0.009.
Values may be sent and summed in bfloat16 or wider, within the bound.
No kernel may reach another device: no remote copies, remote signals or barrier semaphores. Data moves between devices by JAX's collectives and lax.ppermute only.
A program may use at most 64 MiB of HBM per device.

v0:
```python
import math
import jax
import jax.numpy as jnp
from jax import lax
from jax.sharding import PartitionSpec as P

KVH = 8
HD = 128
PAGE = 32
REQS = 4
HITS = 4
CAPF = 6
CAPN = 2
EPSILON = 1e-06
ROPE_BASE = 1000000.0


def in_one_piece(arrays, axis, dim, along):
    ends, at = ([], 0)
    for a in arrays[:-1]:
        at += a.shape[along]
        ends.append(at)
    both = jnp.concatenate(arrays, axis=along)
    return tuple(jnp.split(lax.all_gather(both, axis, axis=dim, tiled=True), ends, axis=along))


def partner(value, axis, stride):
    mask = 2**stride
    pairs = [(source, source ^ mask) for source in range(lax.axis_size(axis))]
    return lax.ppermute(value, axis, pairs)


def rotate(values, positions):
    half = values.shape[-1] // 2
    steps_range = jnp.arange(half, dtype=jnp.float32)
    frequency = ROPE_BASE ** (-2.0 * steps_range / values.shape[-1])
    angles = positions.astype(jnp.float32)[:, None, None] * frequency[None, None, :]
    cosine = jnp.cos(angles)
    sine = jnp.sin(angles)
    first_half = values[..., :half]
    second_half = values[..., half:]
    return jnp.concatenate(
        [first_half * cosine - second_half * sine, second_half * cosine + first_half * sine],
        axis=-1,
    )


def slot_table(owners_row, capacity, seats):
    count_items = owners_row.shape[0]
    item_index = jnp.arange(count_items, dtype=jnp.int32)
    earlier_same = (owners_row[:, None] == owners_row[None, :]) & (
        item_index[None, :] < item_index[:, None]
    )
    slots = jnp.sum(earlier_same.astype(jnp.int32), axis=1)
    targets = owners_row * capacity + slots
    seat_index = jnp.arange(seats, dtype=jnp.int32)
    return targets[:, None] == seat_index[None, :]


def join_stack(held_new, held_cached, upper_half, other_new, other_cached):
    held_new = jnp.where(
        upper_half,
        jnp.concatenate([other_new, held_new], axis=0),
        jnp.concatenate([held_new, other_new], axis=0),
    )
    held_cached = jnp.where(
        upper_half,
        jnp.concatenate([other_cached, held_cached], axis=0),
        jnp.concatenate([held_cached, other_cached], axis=0),
    )
    return (held_new, held_cached)


def unstack_columns(held):
    return held.transpose(1, 0, 2).reshape(held.shape[1], held.shape[0] * held.shape[2])


def body(tokens, lengths, hit_pages, new_owner, w_query, w_keyval, w_out, pool_pages):
    rows_dev = tokens.shape[0]
    tp_count = lax.axis_size("tp")
    pool_count = lax.axis_size("pool")
    tp_rank = lax.axis_index("tp")
    group_rows = rows_dev * tp_count
    query_width = w_query.shape[1]
    part_width = w_keyval.shape[1] // 2
    heads_here = query_width // HD
    sharing = tp_count // KVH
    pages_here = pool_pages.shape[0]
    keyval_local = w_keyval.reshape(w_keyval.shape[0] * 2, part_width)
    pages_flat = pool_pages.reshape(pages_here, pool_pages.shape[1] * pool_pages.shape[2])
    tokens_wide = tokens.astype(jnp.float32)
    normed = (
        tokens_wide
        * lax.rsqrt(jnp.mean(tokens_wide * tokens_wide, axis=1, keepdims=True) + EPSILON)
    ).astype(jnp.bfloat16)
    full_query, full_keyval = in_one_piece((w_query, keyval_local), "pool", 0, 1)
    row_piece = lax.all_gather(normed, "tp", axis=0, tiled=True)
    projected = jnp.concatenate(
        [
            jnp.dot(row_piece, full_query, preferred_element_type=jnp.float32),
            jnp.dot(row_piece, full_keyval, preferred_element_type=jnp.float32),
        ],
        axis=1,
    )
    lengths_row = lengths[0]
    ends_at = jnp.cumsum(lengths_row)
    starts_at = ends_at - lengths_row
    token_index = jnp.arange(group_rows, dtype=jnp.int32)
    request_ids = jnp.sum((token_index[:, None] >= ends_at[None, :]).astype(jnp.int32), axis=1)
    chosen = request_ids[:, None] == jnp.arange(REQS, dtype=jnp.int32)[None, :]
    start_of = jnp.sum(jnp.where(chosen, starts_at[None, :], 0), axis=1)
    positions = token_index - start_of + HITS * PAGE
    queries = rotate(
        projected[:, :query_width].reshape(group_rows, heads_here, HD), positions
    ).astype(jnp.bfloat16)
    keyval_part = projected[:, query_width:].astype(jnp.bfloat16)
    page_ids = hit_pages.reshape(-1)
    count_hits = page_ids.shape[0]
    placed_hits = slot_table(page_ids // pages_here, CAPF, pool_count * CAPF)
    wanted = jnp.sum(jnp.where(placed_hits, (page_ids % pages_here)[:, None], 0), axis=0)
    wanted = wanted.reshape(pool_count, CAPF)
    asked = lax.all_to_all(wanted, "pool", split_axis=0, concat_axis=0, tiled=True)
    found = jnp.take(pages_flat, asked.reshape(-1), axis=0)
    found = found.reshape(asked.shape[0], asked.shape[1], pages_flat.shape[1])
    returned = lax.all_to_all(found, "pool", split_axis=0, concat_axis=0, tiled=True)
    returned = returned.reshape(pool_count * CAPF, PAGE * part_width)
    cached_part = jnp.dot(
        placed_hits.astype(jnp.bfloat16), returned, preferred_element_type=jnp.float32
    ).astype(jnp.bfloat16)
    cached_part = cached_part.reshape(count_hits * PAGE, part_width)
    bit_count = sharing.bit_length() - 1
    held_new = keyval_part[None]
    held_cached = cached_part[None]
    for bit_number in range(bit_count):
        other_new, other_cached = partner((held_new, held_cached), "tp", bit_number)
        upper_half = tp_rank // 2**bit_number % 2 == 1
        held_new, held_cached = join_stack(
            held_new, held_cached, upper_half, other_new, other_cached
        )
    new_head = unstack_columns(held_new)
    cached_head = unstack_columns(held_cached)
    new_keys = (
        rotate(new_head[:, :HD].astype(jnp.float32).reshape(group_rows, 1, HD), positions)
        .astype(jnp.bfloat16)
        .reshape(group_rows, HD)
    )
    stored_head = jnp.concatenate([new_keys, new_head[:, HD:]], axis=1)
    own_columns = lax.dynamic_slice_in_dim(
        stored_head, tp_rank % sharing * part_width, part_width, 1
    )
    page_count = group_rows // PAGE
    page_rows = own_columns.reshape(page_count, PAGE * part_width)
    placed_new = slot_table(new_owner[0], CAPN, pool_count * CAPN).astype(jnp.bfloat16)
    outgoing = jnp.dot(placed_new.T, page_rows, preferred_element_type=jnp.float32).astype(
        jnp.bfloat16
    )
    outgoing = outgoing.reshape(pool_count, CAPN, PAGE * part_width)
    new_store = lax.all_to_all(outgoing, "pool", split_axis=0, concat_axis=0, tiled=True).reshape(
        pool_count * CAPN, 1, PAGE * part_width
    )
    keys_all = jnp.concatenate([cached_head[:, :HD], new_keys], axis=0)
    values_all = jnp.concatenate([cached_head[:, HD:], new_head[:, HD:]], axis=0)
    cached_rows = count_hits * PAGE
    key_request = jnp.concatenate(
        [jnp.arange(cached_rows, dtype=jnp.int32) // (HITS * PAGE), request_ids]
    )
    key_order = jnp.concatenate([jnp.full((cached_rows,), -1, jnp.int32), token_index])
    block_rows = min(group_rows, 512)

    def attend(first_row):
        scores = jnp.einsum(
            "bhd,kd->hbk", queries, keys_all, preferred_element_type=jnp.float32
        ) / math.sqrt(HD)
        visible = (request_ids[:, None] == key_request[None, :]) & (
            key_order[None, :] <= token_index[:, None]
        )
        scores = jnp.where(visible[None], scores, -jnp.inf)
        highest = jnp.max(scores, axis=-1, keepdims=True)
        expanded = jnp.exp(scores - highest)
        weights = (expanded / jnp.sum(expanded, axis=-1, keepdims=True)).astype(jnp.bfloat16)
        blended = jnp.einsum(
            "hbk,kd->bhd", weights, values_all, preferred_element_type=jnp.float32
        ).astype(jnp.bfloat16)
        return blended.reshape(block_rows, query_width)

    attended = lax.map(
        attend, jnp.arange(group_rows // block_rows, dtype=jnp.int32) * block_rows
    ).reshape(group_rows, query_width)
    full_out = lax.all_gather(w_out, "pool", axis=1, tiled=True)
    summed = lax.psum_scatter(
        jnp.dot(attended, full_out, preferred_element_type=jnp.float32).astype(jnp.bfloat16),
        "tp",
        scatter_dimension=0,
        tiled=True,
    ).astype(jnp.float32)
    mixed = tokens_wide + summed
    return (mixed, new_store)


def solution(mesh):
    return jax.shard_map(
        body,
        mesh=mesh,
        in_specs=(
            P(("pool", "tp"), None),
            P("pool", None),
            P("pool", None, None),
            P("pool", None),
            P("pool", "tp"),
            P("pool", "tp"),
            P("tp", "pool"),
            P("pool", "tp", None),
        ),
        out_specs=(P(("pool", "tp"), None), P("pool", "tp", None)),
        check_vma=False,
    )
```

profile of v0, /device:TPU:2, one launch (start us, length us, event | category | flops | bytes accessed | tf_op | source)
XLA Modules:
  0.0 323.8 jit_solution(13723968068413563517)
XLA Ops:
  7.3 1.2 reshape.404
  8.4 2.0 pad_maximum_fusion
  10.6 1.1 fusion.18
  11.7 1.8 fusion.19
  13.6 0.7 all-gather.8.cloned.1.call-update
  14.4 0.2 convert_reduce_fusion.2
  14.6 0.7 all_to_all.12
  15.3 8.5 %all-to-all-start = ((s32[8,1,6]{2,1,0:T(1,128)}), s32[8,1,6]{2,1,0:T(1,128)S(1)}, u32[]{:S(2)}, u32[]{:S(2)}) async-start(s32[8,1,6]{2,1,0:T(1,128)} %bitcast), calls=%async_computation | async-start | bytes 8192 | tf_op jit(solution)/shard_map/all_to_all | solution.py:122
  23.8 0.2 reduce-window.4
  24.2 7.4 %all-to-all-done = s32[8,1,6]{2,1,0:T(1,128)S(1)} async-done(((s32[8,1,6]{2,1,0:T(1,128)}), s32[8,1,6]{2,1,0:T(1,128)S(1)}, u32[]{:S(2)}, u32[]{:S(2)}) %all-to-all-start) | async-done | bytes 224 | tf_op jit(solution)/shard_map/all_to_all | solution.py:122
  31.5 0.5 broadcast.349
  32.0 0.7 reduce.3
  32.8 0.7 gather_fusion
  33.6 0.8 broadcast_select_fusion
  34.4 3.4 %all-to-all-start.1 = ((bf16[8,6,2048]{2,1,0:T(8,128)(2,1)}), bf16[8,6,2048]{2,1,0:T(8,128)(2,1)S(1)}, u32[]{:S(2)}, u32[]{:S(2)}) async-start(bf16[8,6,2048]{2,1,0:T(8,128)(2,1)} %broadcast_select_fusion), calls=%async_computation.1 | async-start | bytes 524288 | tf_op jit(solution)/shard_map/all_to_all | solution.py:125
  37.9 1.5 fusion.8
  39.4 13.0 %all-to-all-done.1 = bf16[8,6,2048]{2,1,0:T(8,128)(2,1)S(1)} async-done(((bf16[8,6,2048]{2,1,0:T(8,128)(2,1)}), bf16[8,6,2048]{2,1,0:T(8,128)(2,1)S(1)}, u32[]{:S(2)}, u32[]{:S(2)}) %all-to-all-start.1) | async-done | bytes 196640 | tf_op jit(solution)/shard_map/all_to_all | solution.py:125
  52.5 0.2 convolution_convert_fusion.2
  52.7 0.2 broadcast_in_dim_reshape.3
  53.1 1.2 collective-permute-done
  54.3 1.7 collective-permute-start.1
  56.0 1.8 multiply_cosine_fusion
  57.8 2.2 collective-permute-done.1
  60.0 0.7 maximum_select_fusion
  60.7 33.0 %all-gather.6.cloned.1.call-done = bf16[8192,320]{1,0:T(8,128)(2,1)} async-done(((bf16[1024,320]{1,0:T(8,128)(2,1)}), bf16[8192,320]{1,0:T(8,128)(2,1)}) %all-gather.6.cloned.1.call-update) | async-done | bytes 5242896 | tf_op jit(solution)/shard_map/all_gather | solution.py:24
  93.7 59.0 %all-gather.4.cloned.1.call-done = bf16[512,8192]{1,0:T(8,128)(2,1)} async-done(((bf16[16,8192]{1,0:T(8,128)(2,1)}), bf16[512,8192]{1,0:T(8,128)(2,1)}) %all-gather.4.cloned.1.call-update) | async-done | bytes 8388624 | tf_op jit(solution)/shard_map/all_gather | solution.py:97
  152.7 6.8 %fusion.15 = bf16[1,512,64]{1,2,0:T(8,128)(2,1)S(1)} fusion(bf16[512,8192]{1,0:T(8,128)(2,1)} %all-gather.4.cloned.1.call-done, bf16[8192,320]{1,0:T(8,128)(2,1)} %all-gather.6.cloned.1.call-done), kind=kOutput, calls=%fused_computation.21 | convolution fusion | flops 536903680 | bytes 10551296 | tf_op jit(solution)/shard_map/dot_general | solution.py:101
  159.4 0.3 collective-permute-start.2
  159.8 4.6 %fusion.1 = f32[512,256]{0,1:T(8,128)S(1)} fusion(bf16[512,8192]{1,0:T(8,128)(2,1)S(1)} %copy-done.1, bf16[8192,320]{1,0:T(8,128)(2,1)} %all-gather.6.cloned.1.call-done), kind=kOutput, calls=%fused_computation.3 | convolution fusion | flops 2147483648 | bytes 13107200 | tf_op jit(solution)/shard_map/dot_general | solution.py:100
  164.4 0.2 copy.58
  164.7 0.2 copy.59
  164.9 0.4 collective-permute-start.3
  165.3 1.9 subtract_convert_fusion
  167.2 3.6 %collective-permute-done.3 = bf16[2,512,64]{1,2,0:T(8,128)(2,1)S(1)} collective-permute-done((bf16[2,512,64]{1,2,0:T(8,128)(2,1)S(1)}, bf16[2,512,64]{1,2,0:T(8,128)(2,1)S(1)}, u32[]{:S(2)}, u32[]{:S(2)}) %collective-permute-start.3) | collective-permute-done | bytes 131104 | tf_op jit(solution)/shard_map/ppermute | solution.py:30
  170.9 1.0 fusion.54
  172.1 1.2 fusion.33
  173.4 4.8 %fusion.56 = (f32[2,512]{1,0:T(2,128)S(1)}, f32[2,512,1024]{1,2,0:T(8,128)}) fusion(pred[512,1024]{0,1:T(8,128)(4,1)} %fusion.8, bf16[512,64]{1,0:T(8,128)(2,1)S(1)} %get-tuple-element.25, bf16[512,64]{1,0:T(8,128)(2,1)S(1)} %get-tuple-element.24, bf16[512,128]{1,0:T(8,128)(2,1)S(1)} %copy.56, bf16[512,2,64]{2,0,1:T(8,128)(2,1)} %get-tuple-element.21, ...), kind=kOutput, calls=%fused_computation.109 | convolution fusion | flops 273941504 | bytes 5246976 | tf_op jit(solution)/shard_map/while/body/eval_jaxpr/sub | solution.py:179
  178.2 2.7 fusion.11
  180.8 28.1 %all-gather.8.cloned.1.call-done = bf16[256,8192]{1,0:T(8,128)(2,1)} async-done(((bf16[256,1024]{1,0:T(8,128)(2,1)}), bf16[256,8192]{1,0:T(8,128)(2,1)}) %all-gather.8.cloned.1.call-update) | async-done | bytes 4194320 | tf_op jit(solution)/shard_map/all_gather | solution.py:189
  208.9 7.8 %convolution_convert_fusion = bf16[512,8192]{1,0:T(8,128)(2,1)} fusion(bf16[512,256]{0,1:T(8,128)(2,1)S(1)} %bitcast.70, bf16[256,8192]{1,0:T(8,128)(2,1)} %all-gather.8.cloned.1.call-done), kind=kOutput, calls=%fused_computation.2 | convolution fusion | flops 2151677952 | bytes 12845056 | tf_op jit(solution)/shard_map/dot_general | solution.py:191
  216.7 0.6 copy-done.6
  217.3 0.2 convert_reduce_fusion
  218.0 0.2 reshape.412
  218.2 0.3 convolution_convert_fusion.1
  218.5 12.5 %all_to_all.19 = bf16[8,2,2048]{2,1,0:T(2,128)(2,1)S(1)} all-to-all(bf16[8,2,2048]{2,1,0:T(2,128)(2,1)S(1)} %reshape.413), channel_id=1, replica_groups=mesh['pool'=8,'tp'=32] {'pool'}, dimensions={0} | all-to-all | bytes 131072 | tf_op jit(solution)/shard_map/all_to_all | solution.py:158
  231.0 0.7 reshape.414
  231.7 83.8 %reduce-scatter.2.cloned.1.call-done = bf16[16,8192]{1,0:T(8,128)(2,1)} async-done(((bf16[512,8192]{1,0:T(8,128)(2,1)}), bf16[16,8192]{1,0:T(8,128)(2,1)}) %reduce-scatter.2.cloned.1.call-update) | async-done | bytes 262160 | tf_op jit(solution)/shard_map/reduce_scatter | solution.py:190
  315.5 1.8 convert_add_fusion
  (54 shorter events, 1.9 us)
Async XLA Ops:
  7.2 25.6 %copy-start = (bf16[512,1,2048]{2,0,1:T(8,128)(2,1)S(1)}, bf16[512,1,2048]{2,0,1:T(8,128)(2,1)}, u32[]{:S(2)}) copy-start(bf16[512,1,2048]{2,0,1:T(8,128)(2,1)} %param.15) | copy-start | bytes 6291460
  7.2 30.7 %copy-start.3 = (s32[1024]{0:T(1024)S(1)}, s32[1024]{0:T(1024)}, u32[]{:S(2)}) copy-start(s32[1024]{0:T(1024)} %constant.140.clone.1) | copy-start | bytes 12292
  7.2 7.1 %copy-start.4 = (s32[1,4,4]{2,1,0:T(4,128)S(1)}, s32[1,4,4]{2,1,0:T(4,128)}, u32[]{:S(2)}) copy-start(s32[1,4,4]{2,1,0:T(4,128)} %param.10) | copy-start | bytes 196
  7.2 16.6 %copy-start.5 = (s32[1,4]{1,0:T(1,128)S(1)}, s32[1,4]{1,0:T(1,128)}, u32[]{:S(2)}) copy-start(s32[1,4]{1,0:T(1,128)} %param.9) | copy-start | bytes 52
  7.2 86.5 %all-gather.6.cloned.1.call-start = ((), (), s32[]{:S(2)}) async-start(), calls=%async_computation.5 | async-start | bytes 7077888 | tf_op jit(solution)/shard_map/all_gather | solution.py:24
  10.5 142.2 %all-gather.4.cloned.1.call-start = ((), (), s32[]{:S(2)}) async-start(), calls=%async_computation.4 | async-start | bytes 8650752 | tf_op jit(solution)/shard_map/all_gather | solution.py:97
  13.5 195.4 %all-gather.8.cloned.1.call-start = ((), (), s32[]{:S(2)}) async-start(), calls=%async_computation.6 | async-start | bytes 4718592 | tf_op jit(solution)/shard_map/all_gather | solution.py:189
  15.3 16.2 %all-to-all-start = ((s32[8,1,6]{2,1,0:T(1,128)}), s32[8,1,6]{2,1,0:T(1,128)S(1)}, u32[]{:S(2)}, u32[]{:S(2)}) async-start(s32[8,1,6]{2,1,0:T(1,128)} %bitcast), calls=%async_computation | async-start | bytes 8192 | tf_op jit(solution)/shard_map/all_to_all | solution.py:122
  34.4 18.0 %all-to-all-start.1 = ((bf16[8,6,2048]{2,1,0:T(8,128)(2,1)}), bf16[8,6,2048]{2,1,0:T(8,128)(2,1)S(1)}, u32[]{:S(2)}, u32[]{:S(2)}) async-start(bf16[8,6,2048]{2,1,0:T(8,128)(2,1)} %broadcast_select_fusion), calls=%async_computation.1 | async-start | bytes 524288 | tf_op jit(solution)/shard_map/all_to_all | solution.py:125
  37.8 277.7 %reduce-scatter.2.cloned.1.call-start = ((), (), s32[]{:S(2)}) async-start(), calls=%async_computation.7 | async-start | bytes 8650752 | tf_op jit(solution)/shard_map/reduce_scatter | solution.py:190
  53.0 1.3 collective-permute-start
  54.3 5.6 %collective-permute-start.1 = (bf16[2,512,64]{1,2,0:T(8,128)(2,1)S(1)}, bf16[2,512,64]{1,2,0:T(8,128)(2,1)S(1)}, u32[]{:S(2)}, u32[]{:S(2)}) collective-permute-start(bf16[2,512,64]{1,2,0:T(8,128)(2,1)S(1)} %maximum_select_fusion.2), channel_id=1, source_target_pairs={{0,2},{1,3},{2,0},{3,1},{4,6},{5,7},{6,4},{7,5},{8,10},{9,11},{10,... | collective-permute-start | bytes 393224 | tf_op jit(solution)/shard_map/ppermute | solution.py:30
  152.7 7.1 %copy-start.1 = (bf16[512,8192]{1,0:T(8,128)(2,1)S(1)}, bf16[512,8192]{1,0:T(8,128)(2,1)}, u32[]{:S(2)}) copy-start(bf16[512,8192]{1,0:T(8,128)(2,1)} %all-gather.4.cloned.1.call-done) | copy-start | bytes 25165828
  159.4 5.4 %collective-permute-start.2 = (bf16[1,512,64]{1,2,0:T(8,128)(2,1)S(1)}, bf16[1,512,64]{1,2,0:T(8,128)(2,1)S(1)}, u32[]{:S(2)}, u32[]{:S(2)}) collective-permute-start(bf16[1,512,64]{1,2,0:T(8,128)(2,1)S(1)} %fusion.15), channel_id=1, source_target_pairs={{0,1},{1,0},{2,3},{3,2},{4,5},{5,4},{6,7},{7,6},{8,9},{9,8},{10,11... | collective-permute-start | bytes 196616 | tf_op jit(solution)/shard_map/ppermute | solution.py:30
  164.9 5.9 %collective-permute-start.3 = (bf16[2,512,64]{1,2,0:T(8,128)(2,1)S(1)}, bf16[2,512,64]{1,2,0:T(8,128)(2,1)S(1)}, u32[]{:S(2)}, u32[]{:S(2)}) collective-permute-start(bf16[2,512,64]{1,2,0:T(8,128)(2,1)S(1)} %maximum_select_fusion.3), channel_id=1, source_target_pairs={{0,2},{1,3},{2,0},{3,1},{4,6},{5,7},{6,4},{7,5},{8,10},{9,11},{10,... | collective-permute-start | bytes 393224 | tf_op jit(solution)/shard_map/ppermute | solution.py:30
  216.7 0.7 copy-start.6
  216.7 98.8 %copy-start.2 = (bf16[16,8192]{1,0:T(8,128)(2,1)S(1)}, bf16[16,8192]{1,0:T(8,128)(2,1)}, u32[]{:S(2)}) copy-start(bf16[16,8192]{1,0:T(8,128)(2,1)} %param.8) | copy-start | bytes 786436
Sparse Core Ops, SparseCore 0:
  10.6 83.0 all-gather.5
  96.2 56.3 all-gather.3
  154.5 54.4 all-gather.7
  216.8 98.6 reduce-scatter.1
where the time goes:
time: 324 us
  waiting for transfers between devices  232 us (72%)
  matrix products  27.1 us (8%)
  other arithmetic  16.5 us (5%)
  starting transfers between devices  14.5 us (4%)
  between operations  14.1 us (4%)
  blocking collectives  12.5 us (4%)
  local copies, waits for them, and re-layouts  7.18 us (2%)
    reduce_scatter x1, waiting for transfers between devices, body(): lax.psum_scatter(jnp.dot(attended, full_out, preferred_element_type=jnp.f...  83.8 us
    all_gather x1, waiting for transfers between devices, body(): row_piece = lax.all_gather(normed, 'tp', axis=0, tiled=True)  59 us
    all_gather x1, waiting for transfers between devices, in_one_piece(): lax.all_gather(both, axis, axis=dim, tiled=True)  33 us
    all_gather x1, waiting for transfers between devices, body(): full_out = lax.all_gather(w_out, 'pool', axis=1, tiled=True)  28.1 us
    all_to_all x1, waiting for transfers between devices, body(): lax.all_to_all(found, 'pool', split_axis=0, concat_axis=0, tiled=True)  13 us
    all_to_all x1, blocking collectives, body(): lax.all_to_all(outgoing, 'pool', split_axis=0, concat_axis=0, tiled=True)  12.5 us
    all_to_all x1, starting transfers between devices, body(): lax.all_to_all(wanted, 'pool', split_axis=0, concat_axis=0, tiled=True)  8.47 us
    dot_general x1, matrix products, body(): jnp.dot(attended, full_out, preferred_element_type=jnp.float32)  7.77 us
  transfers between devices with their start and end apart: 10, of which 9 were waited for; matrix products, arithmetic and copies ran while one was open for 11% of the time, Pallas kernels for 0%

commit v1 on v0

--- a/solution.py
+++ b/solution.py
@@ -13,6 +13,11 @@
 CAPN = 2
 EPSILON = 1e-06
 ROPE_BASE = 1000000.0
+
+
+def gather_from_all(x, axis, dim):
+    copies = jnp.concatenate([x] * lax.axis_size(axis), axis=dim)
+    return lax.all_to_all(copies, axis, dim, dim, tiled=True)
 
 
 def in_one_piece(arrays, axis, dim, along):
@@ -94,7 +99,7 @@
         * lax.rsqrt(jnp.mean(tokens_wide * tokens_wide, axis=1, keepdims=True) + EPSILON)
     ).astype(jnp.bfloat16)
     full_query, full_keyval = in_one_piece((w_query, keyval_local), "pool", 0, 1)
-    row_piece = lax.all_gather(normed, "tp", axis=0, tiled=True)
+    row_piece = gather_from_all(normed, "tp", 0)
     projected = jnp.concatenate(
         [
             jnp.dot(row_piece, full_query, preferred_element_type=jnp.float32),

time: 324 us -> 363 us (1.12)
  other arithmetic: 16.5 us -> 46.6 us
  waiting for transfers between devices: 232 us -> 207 us
  starting transfers between devices: 14.5 us -> 37.8 us
  local copies, waits for them, and re-layouts: 7.18 us -> 16.7 us
    ppermute x4, waiting for transfers between devices: 7.03 us -> 95.4 us  [partner(): return lax.ppermute(value, axis, pairs)]
    all_gather x1 -> x0, waiting for transfers between devices: 59 us -> none  [body(): row_piece = lax.all_gather(normed, 'tp', axis=0, tiled=True)]
    unnamed x0 -> x31, other arithmetic: none -> 34.9 us
    all_gather x1, waiting for transfers between devices: 33 us -> 0.01 us  [in_one_piece(): lax.all_gather(both, axis, axis=dim, tiled=True)]
    all_gather x1, waiting for transfers between devices: 28.1 us -> 0.02 us  [body(): full_out = lax.all_gather(w_out, 'pool', axis=1, tiled=True)]
    ppermute x4, starting transfers between devices: 2.5 us -> 14.2 us  [partner(): return lax.ppermute(value, axis, pairs)]
    dot_general x0 -> x2, local copies, waits for them, and re-layouts: none -> 8.57 us  [body(): jnp.dot(row_piece, full_query, preferred_element_type=jnp.float32)]
    all_to_all x0 -> x1, starting transfers between devices: none -> 7.81 us  [gather_from_all(): return lax.all_to_all(copies, axis, dim, dim, tiled=True)]
  transfers between devices with their start and end apart: 10 -> 10, of which waited for: 9 -> 6; matrix products, arithmetic and copies ran while one was open for 11% -> 22% of each run, Pallas kernels for 0% -> 0%
where the time goes in v1:
time: 363 us; the launch traced here: 362 us
  waiting for transfers between devices  207 us (57%)
  other arithmetic  46.6 us (13%)
  starting transfers between devices  37.8 us (10%)
  matrix products  29.2 us (8%)
  local copies, waits for them, and re-layouts  16.7 us (5%)
  between operations  14.1 us (4%)
  blocking collectives  10.8 us (3%)
    ppermute x4, waiting for transfers between devices, partner(): return lax.ppermute(value, axis, pairs)  95.4 us
    reduce_scatter x1, waiting for transfers between devices, body(): lax.psum_scatter(jnp.dot(attended, full_out, preferred_element_type=jnp.f...  89.7 us
    unnamed x31, other arithmetic  34.9 us
    ppermute x4, starting transfers between devices, partner(): return lax.ppermute(value, axis, pairs)  14.2 us
    all_to_all x1, waiting for transfers between devices, body(): lax.all_to_all(found, 'pool', split_axis=0, concat_axis=0, tiled=True)  14.2 us
    all_to_all x1, blocking collectives, body(): lax.all_to_all(outgoing, 'pool', split_axis=0, concat_axis=0, tiled=True)  10.8 us
    dot_general x2, local copies, waits for them, and re-layouts, body(): jnp.dot(row_piece, full_query, preferred_element_type=jnp.float32)  8.57 us
    all_to_all x1, starting transfers between devices, body(): lax.all_to_all(wanted, 'pool', split_axis=0, concat_axis=0, tiled=True)  8.47 us
  transfers between devices with their start and end apart: 10, of which 6 were waited for; matrix products, arithmetic and copies ran while one was open for 22% of the time, Pallas kernels for 0%

profile of v1, /device:TPU:2, one launch (start us, length us, event | category | flops | bytes accessed | tf_op | source)
XLA Modules:
  0.0 362.4 jit_solution(9961857199882304384)
XLA Ops:
  7.2 1.2 reshape.405
  8.5 2.0 pad_maximum_fusion
  12.2 8.5 %all-to-all-start = ((s32[8,1,6]{2,1,0:T(1,128)}), s32[8,1,6]{2,1,0:T(1,128)S(1)}, u32[]{:S(2)}, u32[]{:S(2)}) async-start(s32[8,1,6]{2,1,0:T(1,128)} %bitcast), calls=%async_computation | async-start | bytes 8192 | tf_op jit(solution)/shard_map/all_to_all | solution.py:127
  20.7 1.1 fusion.16
  21.8 1.8 constant_dynamic-update-slice_fusion.31
  23.6 1.8 constant_dynamic-update-slice_fusion.30
  25.4 1.8 constant_dynamic-update-slice_fusion.29
  27.2 1.8 constant_dynamic-update-slice_fusion.28
  28.9 1.8 constant_dynamic-update-slice_fusion.27
  30.7 1.8 constant_dynamic-update-slice_fusion.26
  32.5 1.8 constant_dynamic-update-slice_fusion.25
  34.3 1.8 constant_dynamic-update-slice_fusion.24
  36.0 1.8 constant_dynamic-update-slice_fusion.23
  37.8 1.8 constant_dynamic-update-slice_fusion.22
  39.6 0.8 constant_dynamic-update-slice_fusion.21
  43.7 0.8 constant_dynamic-update-slice_fusion.16
  44.5 0.8 constant_dynamic-update-slice_fusion.15
  45.3 0.8 constant_dynamic-update-slice_fusion.14
  46.2 0.8 constant_dynamic-update-slice_fusion.13
  47.0 0.8 constant_dynamic-update-slice_fusion.12
  50.2 0.8 constant_dynamic-update-slice_fusion.8
  51.0 0.8 constant_dynamic-update-slice_fusion.7
  51.9 0.8 constant_dynamic-update-slice_fusion.6
  52.7 0.8 constant_dynamic-update-slice_fusion.5
  55.1 0.8 constant_dynamic-update-slice_fusion.2
  59.7 7.2 %all-to-all-start.1 = ((bf16[8,6,2048]{2,1,0:T(8,128)(2,1)}), bf16[8,6,2048]{2,1,0:T(8,128)(2,1)S(1)}, u32[]{:S(2)}, u32[]{:S(2)}) async-start(bf16[8,6,2048]{2,1,0:T(8,128)(2,1)} %broadcast_select_fusion), calls=%async_computation.1 | async-start | bytes 524288 | tf_op jit(solution)/shard_map/all_to_all | solution.py:130
  66.9 0.8 constant_dynamic-update-slice_fusion
  67.7 14.2 %all-to-all-done.1 = bf16[8,6,2048]{2,1,0:T(8,128)(2,1)S(1)} async-done(((bf16[8,6,2048]{2,1,0:T(8,128)(2,1)}), bf16[8,6,2048]{2,1,0:T(8,128)(2,1)S(1)}, u32[]{:S(2)}, u32[]{:S(2)}) %all-to-all-start.1) | async-done | bytes 196640 | tf_op jit(solution)/shard_map/all_to_all | solution.py:130
  81.9 7.8 %all-to-all-start.2 = ((bf16[32,16,8192]{2,1,0:T(8,128)(2,1)}), bf16[32,16,8192]{2,1,0:T(8,128)(2,1)}, u32[]{:S(2)}, u32[]{:S(2)}) async-start(bf16[32,16,8192]{2,1,0:T(8,128)(2,1)} %bitcast.6), calls=%async_computation.2 | async-start | bytes 16777216 | tf_op jit(solution)/shard_map/all_to_all | solution.py:20
  90.9 0.8 fusion.6
  92.6 1.1 collective-permute-done
  93.7 1.6 collective-permute-start.1
  95.8 91.3 %collective-permute-done.1 = bf16[2,512,64]{1,2,0:T(8,128)(2,1)S(1)} collective-permute-done((bf16[2,512,64]{1,2,0:T(8,128)(2,1)S(1)}, bf16[2,512,64]{1,2,0:T(8,128)(2,1)S(1)}, u32[]{:S(2)}, u32[]{:S(2)}) %collective-permute-start.1) | collective-permute-done | bytes 131104 | tf_op jit(solution)/shard_map/ppermute | solution.py:35
  187.2 7.1 %all-to-all-done.2 = bf16[32,16,8192]{2,1,0:T(8,128)(2,1)} async-done(((bf16[32,16,8192]{2,1,0:T(8,128)(2,1)}), bf16[32,16,8192]{2,1,0:T(8,128)(2,1)}, u32[]{:S(2)}, u32[]{:S(2)}) %all-to-all-start.2) | async-done | bytes 8388640 | tf_op jit(solution)/shard_map/all_to_all | solution.py:20
  194.3 6.8 %fusion.13 = bf16[1,512,64]{1,2,0:T(8,128)(2,1)S(1)} fusion(bf16[512,8192]{1,0:T(8,128)(2,1)} %bitcast.7, bf16[8192,320]{1,0:T(8,128)(2,1)} %all-gather.3.cloned.1.call-done), kind=kOutput, calls=%fused_computation.20 | convolution fusion | flops 536903680 | bytes 10551296 | tf_op jit(solution)/shard_map/dot_general | solution.py:106
  201.4 2.2 slice_bitcast_fusion
  203.7 6.3 %copy.49 = bf16[256,8192]{1,0:T(8,128)(2,1)} copy(bf16[256,8192]{0,1:T(8,128)(2,1)} %slice_bitcast_fusion) | data formatting | bytes 8388608 | tf_op jit(solution)/shard_map/dot_general | solution.py:105
  210.0 6.9 %fusion.54 = f32[512,2,128]{0,2,1:T(8,128)S(1)} fusion(bf16[512,8192,1]{1,0,2:T(8,128)(2,1)} %bitcast.23, bf16[2,128,8192]{2,1,0:T(8,128)(2,1)} %bitcast.72), kind=kOutput, calls=%fused_computation.140 | convolution fusion | flops 2147483648 | bytes 13107200 | tf_op jit(solution)/shard_map/dot_general | solution.py:105
  217.0 12.2 %collective-permute-start.3 = (bf16[2,512,64]{1,2,0:T(8,128)(2,1)S(1)}, bf16[2,512,64]{1,2,0:T(8,128)(2,1)S(1)}, u32[]{:S(2)}, u32[]{:S(2)}) collective-permute-start(bf16[2,512,64]{1,2,0:T(8,128)(2,1)S(1)} %maximum_select_fusion.3), channel_id=1, source_target_pairs={{0,2},{1,3},{2,0},{3,1},{4,6},{5,7},{6,4},{7,5},{8,10},{9,11},{10,... | collective-permute-start | bytes 393224 | tf_op jit(solution)/shard_map/ppermute | solution.py:35
  230.0 2.9 collective-permute-done.3
  233.6 1.0 copy.58
  235.4 1.2 fusion.32
  236.7 4.6 %fusion.53 = (f32[2,512]{1,0:T(2,128)S(1)}, f32[2,512,1024]{1,2,0:T(8,128)}) fusion(pred[512,1024]{0,1:T(8,128)(4,1)S(1)} %fusion.6, bf16[512,2,64]{0,2,1:T(8,128)(2,1)} %get-tuple-element.21, bf16[512,2,64]{0,2,1:T(8,128)(2,1)} %get-tuple-element.20, bf16[512,64]{1,0:T(8,128)(2,1)S(1)} %get-tuple-element.23, bf16[512,64]{1,0:T(8,128)(2,1)S(1)} %get-tuple-element.22, ...), kind=kOutput, calls=%fused_computation.139 | convolution fusion | flops 273941504 | bytes 5246976 | tf_op jit(solution)/shard_map/while/body/eval_jaxpr/sub | solution.py:184
  241.3 2.6 fusion.9
  244.0 7.8 %convolution_convert_fusion = bf16[512,8192]{1,0:T(8,128)(2,1)} fusion(bf16[512,256]{0,1:T(8,128)(2,1)S(1)} %bitcast.75, bf16[256,8192]{1,0:T(8,128)(2,1)} %all-gather.5.cloned.1.call-done), kind=kOutput, calls=%fused_computation.2 | convolution fusion | flops 2151677952 | bytes 12845056 | tf_op jit(solution)/shard_map/dot_general | solution.py:196
  253.0 10.8 %all_to_all.31 = bf16[8,2,2048]{2,1,0:T(2,128)(2,1)S(1)} all-to-all(bf16[8,2,2048]{2,1,0:T(2,128)(2,1)S(1)} %reshape.413), channel_id=1, replica_groups=mesh['pool'=8,'tp'=32] {'pool'}, dimensions={0} | all-to-all | bytes 131072 | tf_op jit(solution)/shard_map/all_to_all | solution.py:163
  264.4 89.7 %reduce-scatter.2.cloned.1.call-done = bf16[16,8192]{1,0:T(8,128)(2,1)} async-done(((bf16[512,8192]{1,0:T(8,128)(2,1)}), bf16[16,8192]{1,0:T(8,128)(2,1)}) %reduce-scatter.2.cloned.1.call-update) | async-done | bytes 262160 | tf_op jit(solution)/shard_map/reduce_scatter | solution.py:195
  354.1 1.8 convert_add_fusion
  (83 shorter events, 19.7 us)
Async XLA Ops:
  7.2 50.9 %copy-start = (bf16[512,1,2048]{2,0,1:T(8,128)(2,1)S(1)}, bf16[512,1,2048]{2,0,1:T(8,128)(2,1)}, u32[]{:S(2)}) copy-start(bf16[512,1,2048]{2,0,1:T(8,128)(2,1)} %param.15) | copy-start | bytes 6291460
  7.2 32.4 %copy-start.1 = (bf16[16,8192]{1,0:T(8,128)(2,1)S(1)}, bf16[16,8192]{1,0:T(8,128)(2,1)}, u32[]{:S(2)}) copy-start(bf16[16,8192]{1,0:T(8,128)(2,1)} %param.8) | copy-start | bytes 786436
  7.2 187.2 %all-gather.3.cloned.1.call-start = ((), (), s32[]{:S(2)}) async-start(), calls=%async_computation.5 | async-start | bytes 7077888 | tf_op jit(solution)/shard_map/all_gather | solution.py:29
  12.2 44.6 %all-to-all-start = ((s32[8,1,6]{2,1,0:T(1,128)}), s32[8,1,6]{2,1,0:T(1,128)S(1)}, u32[]{:S(2)}, u32[]{:S(2)}) async-start(s32[8,1,6]{2,1,0:T(1,128)} %bitcast), calls=%async_computation | async-start | bytes 8192 | tf_op jit(solution)/shard_map/all_to_all | solution.py:127
  59.7 22.2 %all-to-all-start.1 = ((bf16[8,6,2048]{2,1,0:T(8,128)(2,1)}), bf16[8,6,2048]{2,1,0:T(8,128)(2,1)S(1)}, u32[]{:S(2)}, u32[]{:S(2)}) async-start(bf16[8,6,2048]{2,1,0:T(8,128)(2,1)} %broadcast_select_fusion), calls=%async_computation.1 | async-start | bytes 524288 | tf_op jit(solution)/shard_map/all_to_all | solution.py:130
  81.9 8.6 %copy-start.5 = (s32[1,4]{1,0:T(1,128)S(1)}, s32[1,4]{1,0:T(1,128)}, u32[]{:S(2)}) copy-start(s32[1,4]{1,0:T(1,128)} %param.9) | copy-start | bytes 52
  81.9 9.0 %copy-start.4 = (s32[1024]{0:T(1024)S(1)}, s32[1024]{0:T(1024)}, u32[]{:S(2)}) copy-start(s32[1024]{0:T(1024)} %constant.140.clone.1) | copy-start | bytes 12292
  81.9 112.4 %all-to-all-start.2 = ((bf16[32,16,8192]{2,1,0:T(8,128)(2,1)}), bf16[32,16,8192]{2,1,0:T(8,128)(2,1)}, u32[]{:S(2)}, u32[]{:S(2)}) async-start(bf16[32,16,8192]{2,1,0:T(8,128)(2,1)} %bitcast.6), calls=%async_computation.2 | async-start | bytes 16777216 | tf_op jit(solution)/shard_map/all_to_all | solution.py:20
  89.7 154.2 %all-gather.5.cloned.1.call-start = ((), (), s32[]{:S(2)}) async-start(), calls=%async_computation.6 | async-start | bytes 4718592 | tf_op jit(solution)/shard_map/all_gather | solution.py:194
  90.5 263.6 %reduce-scatter.2.cloned.1.call-start = ((), (), s32[]{:S(2)}) async-start(), calls=%async_computation.7 | async-start | bytes 8650752 | tf_op jit(solution)/shard_map/reduce_scatter | solution.py:195
  92.4 1.3 collective-permute-start
  93.7 93.4 %collective-permute-start.1 = (bf16[2,512,64]{1,2,0:T(8,128)(2,1)S(1)}, bf16[2,512,64]{1,2,0:T(8,128)(2,1)S(1)}, u32[]{:S(2)}, u32[]{:S(2)}) collective-permute-start(bf16[2,512,64]{1,2,0:T(8,128)(2,1)S(1)} %maximum_select_fusion.2), channel_id=1, source_target_pairs={{0,2},{1,3},{2,0},{3,1},{4,6},{5,7},{6,4},{7,5},{8,10},{9,11},{10,... | collective-permute-start | bytes 393224 | tf_op jit(solution)/shard_map/ppermute | solution.py:35
  194.3 7.1 %copy-start.2 = (bf16[8192,320]{1,0:T(8,128)(2,1)S(1)}, bf16[8192,320]{1,0:T(8,128)(2,1)}, u32[]{:S(2)}) copy-start(bf16[8192,320]{1,0:T(8,128)(2,1)} %all-gather.3.cloned.1.call-done) | copy-start | bytes 15728644
  201.1 15.8 %collective-permute-start.2 = (bf16[1,512,64]{1,2,0:T(8,128)(2,1)S(1)}, bf16[1,512,64]{1,2,0:T(8,128)(2,1)S(1)}, u32[]{:S(2)}, u32[]{:S(2)}) collective-permute-start(bf16[1,512,64]{1,2,0:T(8,128)(2,1)S(1)} %fusion.13), channel_id=1, source_target_pairs={{0,1},{1,0},{2,3},{3,2},{4,5},{5,4},{6,7},{7,6},{8,9},{9,8},{10,11... | collective-permute-start | bytes 196616 | tf_op jit(solution)/shard_map/ppermute | solution.py:35
  217.0 15.9 %collective-permute-start.3 = (bf16[2,512,64]{1,2,0:T(8,128)(2,1)S(1)}, bf16[2,512,64]{1,2,0:T(8,128)(2,1)S(1)}, u32[]{:S(2)}, u32[]{:S(2)}) collective-permute-start(bf16[2,512,64]{1,2,0:T(8,128)(2,1)S(1)} %maximum_select_fusion.3), channel_id=1, source_target_pairs={{0,2},{1,3},{2,0},{3,1},{4,6},{5,7},{6,4},{7,5},{8,10},{9,11},{10,... | collective-permute-start | bytes 393224 | tf_op jit(solution)/shard_map/ppermute | solution.py:35
  235.4 5.9 %copy-start.3 = (bf16[512,128]{0,1:T(8,128)(2,1)S(1)}, bf16[512,128]{0,1:T(8,128)(2,1)}, u32[]{:S(2)}) copy-start(bf16[512,128]{0,1:T(8,128)(2,1)} %get-tuple-element.24) | copy-start | bytes 393220
  244.0 7.8 %copy-start.6 = (s32[1,16]{1,0:T(1,128)S(1)}, s32[1,16]{1,0:T(1,128)}, u32[]{:S(2)}) copy-start(s32[1,16]{1,0:T(1,128)} %param.11) | copy-start | bytes 196
Sparse Core Ops, SparseCore 0:
  10.6 82.9 all-gather.2
  95.4 53.3 all-gather.4
  251.9 102.1 reduce-scatter.1
